TPU v7x, 32 devices: a whole 2x2x4 slice. The times are simulated.
32 devices in a mesh: seq: 8 (over y, x, core), exp: 4 (over z).
Axes of the slice: x: 2, y: 2, z: 4, core: 2. Of those that a mesh axis runs over, the one named last changes fastest.
Arguments:
- layer_input: bfloat16 [4, 4096, 768], P('exp', 'seq'), may hold values from -6 to 6
- token_ids: int32 [4, 4096], P('exp', 'seq'), may hold values from 0 to 8007, as said below
- segment_ids: int32 [4, 4096], P('exp'), may hold values from 0 to 7, never falling along the last dimension, each value on 1 to 1024 neighbouring positions
- hash_table: int32 [8008], replicated, may hold values from 0 to 3, as said below
- first_gain: float32 [768], replicated, may hold values from 0.25 to 1.75
- first_bias: float32 [768], replicated, may hold values from -1.5 to 1.5
- second_gain: float32 [768], replicated, may hold values from 0.25 to 1.75
- second_bias: float32 [768], replicated, may hold values from -1.5 to 1.5
- w_qkv: bfloat16 [768, 2304], replicated, may hold values from -0.21875 to 0.21875
- w_out: bfloat16 [768, 768], replicated, may hold values from -3 to 3
- w_up: bfloat16 [4, 768, 3072], P('exp'), may hold values from -0.21875 to 0.21875
- w_down: bfloat16 [4, 3072, 768], P('exp'), may hold values from -0.109375 to 0.109375
- cotangent: bfloat16 [4, 4096, 768], P('exp', 'seq'), may hold values from -6 to 6
Outputs:
- layer_output: bfloat16 [4, 4096, 768], P('exp', 'seq')
- grad_input: float32 [4, 4096, 768], P('exp', 'seq')
- grad_w_qkv: float32 [768, 2304], replicated
- grad_w_out: float32 [768, 768], replicated
- grad_first_gain: float32 [768], replicated
- grad_first_bias: float32 [768], replicated
- grad_second_gain: float32 [768], replicated
- grad_second_bias: float32 [768], replicated
- grad_w_up: float32 [4, 768, 3072], P('exp')
- grad_w_down: float32 [4, 3072, 768], P('exp')
Inputs may be any that keep to these rules, and one draw needn't show every extreme that they name: `token_ids`: token ids range over the vocabulary. Among the 512 positions that one device holds, hash_table sends exactly 256 to one expert, the same expert on all devices that hold the same positions of their sequences, and the other experts' counts differ from one another by at most one. `hash_table`: every expert is named by 2002 token ids. `segment_ids`: numbers never fall along a sequence; each document holds 1 to 1024 neighbouring positions, and one in every sequence holds exactly 1024.
All inputs are finite; a program needn't handle non-finite values.
Results may differ from a plain program's by a relative error of at most 0.017.
Values may be sent and summed in bfloat16 or wider, within the bound.
No kernel may reach another device: no remote copies, remote signals or barrier semaphores. Data moves between devices by JAX's collectives and lax.ppermute only.
A program may use at most 192 MiB of HBM per device.

v0:
```python
import math
import jax
import jax.numpy as jnp
from jax import lax
from jax.sharding import PartitionSpec as P

HEADS = 12
HEAD_DIM = 64
DOC_MOST = 1024
NEG_BIG = -1e30
EPSILON = 1e-05


def passed_along(block, axis, distance):
    devices = range(lax.axis_size(axis))
    route = [(i - distance, i) for i in devices if i - distance in devices]
    return lax.ppermute(block, axis, route)


def smooth_gate(values):
    return jax.nn.gelu(values, approximate=True)


def norm_rows(values):
    center = values - jnp.mean(values, axis=-1, keepdims=True)
    scale = lax.rsqrt(jnp.mean(center * center, axis=-1, keepdims=True) + EPSILON)
    return (center * scale, scale)


def norm_back(grad_normed, normed, scale):
    inner = jnp.mean(grad_normed * normed, axis=-1, keepdims=True)
    return scale * (grad_normed - jnp.mean(grad_normed, axis=-1, keepdims=True) - normed * inner)


def over_blocks(step, state, pieces, first):
    length = pieces[0].shape[0]
    stride = math.gcd(length, 512)

    def advance(index, current):
        begin = index * stride
        parts = tuple((piece for piece in pieces))
        return step(current, parts, first + begin)

    return lax.fori_loop(0, length // stride, advance, state)


def allowed_pairs(query_pos, query_seg, key_pos, key_seg, limit):
    inside = (key_pos[None, :] >= 0) & (query_pos[:, None] < limit)
    return (
        inside & (key_pos[None, :] <= query_pos[:, None]) & (key_seg[None, :] == query_seg[:, None])
    )


def head_split(rows):
    return rows.reshape(rows.shape[0], HEADS, HEAD_DIM)


def forward_step(queries, query_pos, query_seg, segment_row, limit):
    width = HEADS * HEAD_DIM
    scale = HEAD_DIM ** (-0.5)

    def step(state, parts, first):
        run_max, run_total, weighted = state
        count = parts[0].shape[0]
        key_rows = head_split(parts[0][:, :width])
        value_rows = head_split(parts[0][:, width:])
        key_pos = first + jnp.arange(count, dtype=jnp.int32)
        key_seg = lax.dynamic_slice_in_dim(segment_row, first, count, 0)
        allowed = allowed_pairs(query_pos, query_seg, key_pos, key_seg, limit)[None]
        scores = (
            jnp.einsum("qhd,khd->hqk", queries, key_rows, preferred_element_type=jnp.float32)
            * scale
        )
        new_max = jnp.maximum(run_max, jnp.max(jnp.where(allowed, scores, NEG_BIG), axis=-1))
        shares = jnp.where(allowed, jnp.exp(scores - new_max[..., None]), 0.0)
        factor = jnp.exp(run_max - new_max)
        run_total = run_total * factor + jnp.sum(shares, axis=-1)
        update = jnp.einsum(
            "hqk,khd->qhd",
            shares.astype(jnp.bfloat16),
            value_rows,
            preferred_element_type=jnp.float32,
        )
        weighted = weighted * factor.T[:, :, None] + update
        return (new_max, run_total, weighted)

    return step


def backward_core(queries, grad_heads, log_total, delta, key_rows, value_rows, allowed):
    scale = HEAD_DIM ** (-0.5)
    scores = (
        jnp.einsum("qhd,khd->hqk", queries, key_rows, preferred_element_type=jnp.float32) * scale
    )
    soft = jnp.where(allowed[None], jnp.exp(scores - log_total[..., None]), 0.0)
    grad_soft = jnp.einsum(
        "qhd,khd->hqk", grad_heads, value_rows, preferred_element_type=jnp.float32
    )
    grad_scores = (soft * (grad_soft - delta[..., None])).astype(jnp.bfloat16)
    return (soft.astype(jnp.bfloat16), grad_scores)


def query_step(queries, grad_heads, log_total, delta, query_pos, query_seg, segment_row, limit):
    width = HEADS * HEAD_DIM
    scale = HEAD_DIM ** (-0.5)

    def step(state, parts, first):
        count = parts[0].shape[0]
        key_rows = head_split(parts[0][:, :width])
        value_rows = head_split(parts[0][:, width:])
        key_pos = first + jnp.arange(count, dtype=jnp.int32)
        key_seg = lax.dynamic_slice_in_dim(segment_row, first, count, 0)
        allowed = allowed_pairs(query_pos, query_seg, key_pos, key_seg, limit)
        soft_low, grad_scores = backward_core(
            queries, grad_heads, log_total, delta, key_rows, value_rows, allowed
        )
        grad_query = (
            jnp.einsum("hqk,khd->qhd", grad_scores, key_rows, preferred_element_type=jnp.float32)
            * scale
        )
        grad_q, grad_block = state
        grad_keys = (
            jnp.einsum("hqk,qhd->khd", grad_scores, queries, preferred_element_type=jnp.float32)
            * scale
        )
        grad_values = jnp.einsum(
            "hqk,qhd->khd", soft_low, grad_heads, preferred_element_type=jnp.float32
        )
        joined = jnp.concatenate(
            [grad_keys.reshape(count, width), grad_values.reshape(count, width)], axis=1
        )
        current = grad_block
        grad_block = current + joined
        return (grad_q + grad_query, grad_block)

    return step


def on_device(
    layer_input,
    token_ids,
    segment_ids,
    hash_table,
    first_gain,
    first_bias,
    second_gain,
    second_bias,
    w_qkv,
    w_out,
    w_up,
    w_down,
    cotangent,
):
    local_len = layer_input.shape[1]
    width = layer_input.shape[2]
    sources = lax.axis_size("exp")
    local_exp = w_up.shape[0]
    experts_total = local_exp * sources
    capacity = 2 * local_len // experts_total
    total_len = local_len * lax.axis_size("seq")
    reach_blocks = (DOC_MOST + local_len - 2) // local_len
    offset = lax.axis_index("seq") * local_len
    segment_row = segment_ids[0]
    query_pos = offset + jnp.arange(local_len, dtype=jnp.int32)
    query_seg = lax.dynamic_slice_in_dim(segment_row, offset, local_len, 0)
    inputs = layer_input[0].astype(jnp.float32)
    normed_one, scale_one = norm_rows(inputs)
    attn_in = (normed_one * first_gain + first_bias).astype(jnp.bfloat16)
    projected = jnp.dot(attn_in, w_qkv, preferred_element_type=jnp.float32).astype(jnp.bfloat16)
    queries = head_split(projected[:, :width])
    key_value = projected[:, width:]
    kv_blocks = [key_value]
    moving = key_value
    for hop_index in range(reach_blocks):
        moving = passed_along(moving, "seq", 1)
        kv_blocks.append(moving)
    state = (
        jnp.full((HEADS, local_len), NEG_BIG, jnp.float32),
        jnp.zeros((HEADS, local_len), jnp.float32),
        jnp.zeros((local_len, HEADS, HEAD_DIM), jnp.float32),
    )
    attend = forward_step(queries, query_pos, query_seg, segment_row, total_len)
    for block_index in range(reach_blocks + 1):
        state = over_blocks(
            attend, state, (kv_blocks[block_index],), offset - block_index * local_len
        )
    run_max, run_total, weighted = state
    attn_exact = (weighted / run_total.T[:, :, None]).reshape(local_len, width)
    log_total = run_max + jnp.log(run_total)
    attn_rows = attn_exact.astype(jnp.bfloat16)
    resid = inputs + jnp.dot(attn_rows, w_out, preferred_element_type=jnp.float32)
    normed_two, scale_two = norm_rows(resid)
    ffn_in = (normed_two * second_gain + second_bias).astype(jnp.bfloat16)
    choice_ids = hash_table[token_ids[0]]
    order = jnp.argsort(choice_ids, stable=True)
    places = jnp.argsort(order, stable=True)
    expert_grid = jnp.arange(experts_total, dtype=jnp.int32)
    matches = choice_ids[:, None] == expert_grid[None, :]
    counts = jnp.sum(matches.astype(jnp.int32), axis=0)
    starts = jnp.cumsum(counts) - counts
    slot_grid = jnp.arange(capacity, dtype=jnp.int32)
    gather_index = order[jnp.minimum(starts[:, None] + slot_grid[None, :], local_len - 1)]
    filled = (slot_grid[None, :] < counts[:, None])[:, :, None]
    own_start = jnp.sum(jnp.where(matches, starts[None, :], 0), axis=1)
    token_slot = choice_ids * capacity + places - own_start
    send = jnp.where(filled, ffn_in[gather_index], jnp.zeros((), jnp.bfloat16))
    received = lax.all_to_all(send, "exp", split_axis=0, concat_axis=0, tiled=True)
    grouped = received.reshape(sources, local_exp, capacity, width)
    pre_act = jnp.einsum("secd,edf->secf", grouped, w_up, preferred_element_type=jnp.float32)
    activated, gate_pullback = jax.vjp(smooth_gate, pre_act)
    hidden = activated.astype(jnp.bfloat16)
    expert_out = jnp.einsum(
        "secf,efd->secd", hidden, w_down, preferred_element_type=jnp.float32
    ).astype(jnp.bfloat16)
    returned = lax.all_to_all(
        expert_out.reshape(experts_total, capacity, width),
        "exp",
        split_axis=0,
        concat_axis=0,
        tiled=True,
    )
    ffn_rows = returned.reshape(experts_total * capacity, width)[token_slot].astype(jnp.float32)
    layer_output = (resid + ffn_rows).astype(jnp.bfloat16)
    grad_final = cotangent[0].astype(jnp.float32)
    grad_branch = grad_final.astype(jnp.bfloat16)
    grad_send = jnp.where(filled, grad_branch[gather_index], jnp.zeros((), jnp.bfloat16))
    grad_received = lax.all_to_all(
        grad_send, "exp", split_axis=0, concat_axis=0, tiled=True
    ).reshape(sources, local_exp, capacity, width)
    grad_w_down = jnp.einsum(
        "secf,secd->efd", hidden, grad_received, preferred_element_type=jnp.float32
    )
    grad_hidden = jnp.einsum(
        "secd,efd->secf", grad_received, w_down, preferred_element_type=jnp.float32
    )
    grad_pre = gate_pullback(grad_hidden)[0].astype(jnp.bfloat16)
    grad_w_up = jnp.einsum("secd,secf->edf", grouped, grad_pre, preferred_element_type=jnp.float32)
    grad_slots = jnp.einsum(
        "secf,edf->secd", grad_pre, w_up, preferred_element_type=jnp.float32
    ).astype(jnp.bfloat16)
    grad_back = lax.all_to_all(
        grad_slots.reshape(experts_total, capacity, width),
        "exp",
        split_axis=0,
        concat_axis=0,
        tiled=True,
    )
    grad_ffn_in = grad_back.reshape(experts_total * capacity, width)[token_slot].astype(jnp.float32)
    grad_second_gain = jnp.sum(grad_ffn_in * normed_two, axis=0)
    grad_second_bias = jnp.sum(grad_ffn_in, axis=0)
    grad_resid = grad_final + norm_back(grad_ffn_in * second_gain, normed_two, scale_two)
    grad_attn = grad_resid.astype(jnp.bfloat16)
    grad_w_out = jnp.einsum("cd,ce->de", attn_rows, grad_attn, preferred_element_type=jnp.float32)
    grad_out_rows = jnp.einsum(
        "ce,de->cd", grad_attn, w_out, preferred_element_type=jnp.float32
    ).astype(jnp.bfloat16)
    grad_heads = head_split(grad_out_rows)
    delta = jnp.sum(grad_heads.astype(jnp.float32) * head_split(attn_exact), axis=-1).T
    back_blocks = [key_value]
    moving = key_value
    for hop_index in range(reach_blocks):
        moving = passed_along(moving, "seq", 1)
        back_blocks.append(moving)
    grad_query = jnp.zeros((local_len, HEADS, HEAD_DIM), jnp.float32)
    block_grads = []
    for block_index in range(reach_blocks + 1):
        base = offset - block_index * local_len
        back_step = query_step(
            queries, grad_heads, log_total, delta, query_pos, query_seg, segment_row, total_len
        )
        grad_query, grad_block = over_blocks(
            back_step,
            (grad_query, jnp.zeros((local_len, 2 * width), jnp.float32)),
            (back_blocks[block_index],),
            base,
        )
        block_grads.append(grad_block)
    carried = block_grads[reach_blocks]
    for block_index in range(reach_blocks, 0, -1):
        carried = (
            passed_along(carried.astype(jnp.bfloat16), "seq", -1).astype(carried.dtype)
            + block_grads[block_index - 1]
        )
    grad_proj = jnp.concatenate([grad_query.reshape(local_len, width), carried], axis=1).astype(
        jnp.bfloat16
    )
    grad_w_qkv = jnp.einsum("cd,ce->de", attn_in, grad_proj, preferred_element_type=jnp.float32)
    grad_attn_in = jnp.einsum("ce,de->cd", grad_proj, w_qkv, preferred_element_type=jnp.float32)
    grad_first_gain = jnp.sum(grad_attn_in * normed_one, axis=0)
    grad_first_bias = jnp.sum(grad_attn_in, axis=0)
    grad_input = grad_resid + norm_back(grad_attn_in * first_gain, normed_one, scale_one)
    dense = lax.psum(
        (
            grad_w_qkv,
            grad_w_out,
            grad_first_gain,
            grad_first_bias,
            grad_second_gain,
            grad_second_bias,
        ),
        ("seq", "exp"),
    )
    expert_sums = (
        lax.psum(grad_w_up.astype(jnp.bfloat16), "seq").astype(jnp.float32),
        lax.psum(grad_w_down.astype(jnp.bfloat16), "seq").astype(jnp.float32),
    )
    return (
        layer_output[None],
        grad_input[None],
        dense[0],
        dense[1],
        dense[2],
        dense[3],
        dense[4],
        dense[5],
        expert_sums[0],
        expert_sums[1],
    )


def solution(mesh):
    in_specs = (
        P("exp", "seq", None),
        P("exp", "seq"),
        P("exp", None),
        P(),
        P(),
        P(),
        P(),
        P(),
        P(),
        P(),
        P("exp", None, None),
        P("exp", None, None),
        P("exp", "seq", None),
    )
    out_specs = (
        P("exp", "seq", None),
        P("exp", "seq", None),
        P(),
        P(),
        P(),
        P(),
        P(),
        P(),
        P("exp", None, None),
        P("exp", None, None),
    )
    return jax.shard_map(
        on_device, mesh=mesh, in_specs=in_specs, out_specs=out_specs, check_vma=False
    )
```

profile of v0, /device:TPU:0, one launch (start us, length us, event | category | flops | bytes accessed | tf_op | source)
XLA Modules:
  0.0 691.7 jit_solution(2766946564341442537)
XLA Ops:
  10.2 3.3 convolution_convert_fusion
  16.2 3.6 collective-permute-start
  19.8 3.4 gather_fusion
  23.9 3.8 sort.31
  27.7 11.3 %gather_fusion.1 = s32[1024]{0:T(1024)} fusion(s32[512]{0:T(512)S(1)} %get-tuple-element.163, s32[1024]{0:T(1024)S(1)} %broadcast_clamp_fusion.1), kind=kCustom, calls=%fused_computation.1 | custom fusion | bytes 12288 | tf_op jit(solution)/shard_map/gather | solution.py:202
  40.5 3.1 fusion.155
  45.9 4.5 collective-permute-start.1
  56.3 2.3 copy.84
  58.6 7.0 %gather_fusion.4 = bf16[1024,768]{1,0:T(8,128)(2,1)} fusion(bf16[512,768]{1,0:T(8,128)(2,1)} %bitcast.289, s32[1024]{0:T(1024)S(1)} %broadcast_clamp_fusion), kind=kCustom, calls=%fused_computation.4 | custom fusion | bytes 3149824 | tf_op jit(solution)/shard_map/gather | solution.py:226
  65.6 8.6 %select_reduce_fusion.2 = (f32[12,512]{1,0:T(8,128)}, f32[12,512,512]{1,2,0:T(8,128)}) fusion(pred[512,512]{0,1:T(8,128)(4,1)} %get-tuple-element.239, bf16[512,12,64]{0,2,1:T(8,128)(2,1)} %bitcast.294, bf16[512,12,64]{0,2,1:T(8,128)(2,1)} %bitcast.302), kind=kOutput, calls=%fused_computation.33 | convolution fusion | flops 412084224 | bytes 14442496 | tf_op jit(solution)/shard_map/while/body/eval_jaxpr/qhd,khd->hqk/dot_general | solution.py:71
  74.2 2.6 fusion.157
  79.1 2.3 copy.89
  81.5 8.6 %select_reduce_fusion.1 = (f32[12,512]{1,0:T(8,128)}, f32[12,512,512]{1,2,0:T(8,128)}) fusion(pred[512,512]{0,1:T(8,128)(4,1)} %get-tuple-element.241, bf16[512,12,64]{0,2,1:T(8,128)(2,1)} %bitcast.295, bf16[512,12,64]{0,2,1:T(8,128)(2,1)} %bitcast.300), kind=kOutput, calls=%fused_computation.31 | convolution fusion | flops 412084224 | bytes 14442496 | tf_op jit(solution)/shard_map/while/body/eval_jaxpr/qhd,khd->hqk/dot_general | solution.py:71
  90.1 2.6 fusion.156
  97.3 8.1 %select_reduce_fusion = (f32[12,512]{1,0:T(8,128)S(1)}, f32[12,512,512]{1,2,0:T(8,128)}) fusion(pred[512,512]{0,1:T(8,128)(4,1)} %get-tuple-element.240, bf16[512,12,64]{0,2,1:T(8,128)(2,1)} %bitcast.296, bf16[512,12,64]{0,2,1:T(8,128)(2,1)} %bitcast.304), kind=kOutput, calls=%fused_computation.29 | convolution fusion | flops 412084224 | bytes 14442496 | tf_op jit(solution)/shard_map/while/body/eval_jaxpr/qhd,khd->hqk/dot_general | solution.py:71
  106.1 7.3 %fusion.13 = f32[12,512]{1,0:T(8,128)S(1)} fusion(f32[12,512,512]{1,2,0:T(8,128)} %get-tuple-element.247, f32[12,512]{1,0:T(8,128)S(1)} %get-tuple-element.210, pred[512,512]{0,1:T(8,128)(4,1)S(1)} %copy-done.19), kind=kLoop, calls=%fused_computation.36 | loop fusion | flops 12576768 | bytes 12894208 | tf_op jit(solution)/shard_map/while/body/eval_jaxpr/reduce_sum | solution.py:77
  113.4 20.8 %fusion.36 = f32[12,64,512]{2,1,0:T(8,128)} fusion(bf16[512,12,64]{0,2,1:T(8,128)(2,1)} %bitcast.324, f32[12,512,512]{1,2,0:T(8,128)} %get-tuple-element.247, f32[12,512]{1,0:T(8,128)S(1)} %get-tuple-element.210, pred[512,512]{0,1:T(8,128)(4,1)} %get-tuple-element.241), kind=kOutput, calls=%fused_computation.57 | convolution fusion | flops 415236096 | bytes 15228928 | tf_op jit(solution)/shard_map/while/body/eval_jaxpr/hqk,khd->qhd/dot_general | solution.py:78
  134.2 3.5 fusion.11
  137.8 4.7 fusion.38
  142.5 7.3 %fusion.15 = f32[12,512]{1,0:T(8,128)S(1)} fusion(f32[12,512,512]{1,2,0:T(8,128)} %get-tuple-element.245, f32[12,512]{1,0:T(8,128)} %get-tuple-element.196, pred[512,512]{0,1:T(8,128)(4,1)} %get-tuple-element.240), kind=kLoop, calls=%fused_computation.38 | loop fusion | flops 12576768 | bytes 12894208 | tf_op jit(solution)/shard_map/while/body/eval_jaxpr/reduce_sum | solution.py:77
  150.0 8.8 %fusion.158 = (bf16[512,12,64]{0,2,1:T(8,128)(2,1)S(1)}, f32[512,12,64]{0,2,1:T(8,128)}) fusion(f32[512,12]{0,1:T(8,128)S(1)} %get-tuple-element.194, bf16[512,12,64]{0,2,1:T(8,128)(2,1)S(1)} %bitcast.326, f32[12,512,512]{1,2,0:T(8,128)} %get-tuple-element.245, f32[12,512]{1,0:T(8,128)S(1)} %copy-done.37, pred[512,512]{0,1:T(8,128)(4,1)S(1)} %copy-done.21, ...), kind=kOutput, calls=%fused_computation.216 | convolution fusion | flops 417988608 | bytes 19259392 | tf_op jit(solution)/shard_map/while/body/eval_jaxpr/hqk,khd->qhd/dot_general | solution.py:78
  162.6 7.0 %gather_fusion.2 = bf16[1024,768]{1,0:T(8,128)(2,1)} fusion(bf16[512,768]{1,0:T(8,128)(2,1)} %add_convert_fusion.1, s32[1024]{0:T(1024)} %copy-done.44), kind=kCustom, calls=%fused_computation.2 | custom fusion | bytes 3149824 | tf_op jit(solution)/shard_map/gather | solution.py:206
  169.7 3.8 broadcast_select_fusion
  173.5 4.9 all-to-all-start
  179.0 4.4 sort.32
  186.3 28.2 %all-to-all-done = bf16[4,256,768]{2,1,0:T(8,128)(2,1)} async-done(((bf16[4,256,768]{2,1,0:T(8,128)(2,1)}), bf16[4,256,768]{2,1,0:T(8,128)(2,1)}, u32[]{:S(2)}, u32[]{:S(2)}) %all-to-all-start) | async-done | bytes 1572896 | tf_op jit(solution)/shard_map/all_to_all | solution.py:207
  214.5 4.4 all-to-all-start.2
  218.9 7.4 %fusion.54 = f32[4,256,3072]{2,1,0:T(8,128)S(1)} fusion(bf16[4,256,768]{2,1,0:T(8,128)(2,1)} %all-to-all-done, bf16[1,768,3072]{2,1,0:T(8,128)(2,1)} %param.23), kind=kOutput, calls=%fused_computation.69 | convolution fusion | flops 4831838208 | bytes 18874368 | tf_op jit(solution)/shard_map/secd,edf->secf/dot_general | solution.py:209
  226.3 4.5 copy-done.64
  230.7 10.8 %fusion.77 = bf16[4,256,768]{2,1,0:T(8,128)(2,1)} fusion(bf16[1,3072,768]{2,1,0:T(8,128)(2,1)} %param.24, f32[4,256,3072]{2,1,0:T(8,128)S(1)} %fusion.54), kind=kOutput, calls=%fused_computation.95 | convolution fusion | flops 4860936192 | bytes 18874368 | tf_op jit(solution)/shard_map/secf,efd->secd/dot_general | solution.py:212
  241.5 13.9 %all-to-all-done.2 = bf16[4,256,768]{2,1,0:T(8,128)(2,1)} async-done(((bf16[4,256,768]{2,1,0:T(8,128)(2,1)}), bf16[4,256,768]{2,1,0:T(8,128)(2,1)}, u32[]{:S(2)}, u32[]{:S(2)}) %all-to-all-start.2) | async-done | bytes 1572896 | tf_op jit(solution)/shard_map/all_to_all | solution.py:227
  255.4 4.8 all-to-all-start.1
  260.2 15.3 %fusion.6 = bf16[4,1,256,3072]{3,2,0,1:T(8,128)(2,1)S(1)} fusion(f32[4,256,3072]{2,1,0:T(8,128)} %copy-done.64, bf16[4,256,768]{2,1,0:T(8,128)(2,1)} %all-to-all-done.2, bf16[1,3072,768]{2,1,0:T(8,128)(2,1)} %param.24), kind=kOutput, calls=%fused_computation.14 | convolution fusion | flops 4894752768 | bytes 25165824 | tf_op jit(solution)/shard_map/secd,efd->secf/dot_general | solution.py:233
  275.5 8.5 %fusion.82 = bf16[4,256,768]{2,1,0:T(8,128)(2,1)} fusion(bf16[1,768,3072]{2,1,0:T(8,128)(2,1)} %param.23, bf16[4,1,256,3072]{3,2,0,1:T(8,128)(2,1)S(1)} %fusion.6), kind=kOutput, calls=%fused_computation.96 | convolution fusion | flops 4832624640 | bytes 12582912 | tf_op jit(solution)/shard_map/secf,edf->secd/dot_general | solution.py:238
  284.1 8.2 %fusion.56 = bf16[1,768,3072]{2,1,0:T(8,128)(2,1)} fusion(bf16[4,256,768]{2,1,0:T(8,128)(2,1)} %all-to-all-done, bf16[4,1,256,3072]{3,2,0,1:T(8,128)(2,1)S(1)} %fusion.6), kind=kOutput, calls=%fused_computation.71 | convolution fusion | flops 4834197504 | bytes 12582912 | tf_op jit(solution)/shard_map/secd,secf->edf/dot_general | solution.py:237
  292.3 4.4 all-to-all-done.1
  296.7 4.4 all-to-all-start.3
  301.1 12.0 %fusion.59 = bf16[1,3072,768]{2,1,0:T(8,128)(2,1)} fusion(bf16[4,256,768]{2,1,0:T(8,128)(2,1)} %all-to-all-done.2, f32[4,256,3072]{2,1,0:T(8,128)} %copy-done.64), kind=kOutput, calls=%fused_computation.72 | convolution fusion | flops 4862509056 | bytes 18874368 | tf_op jit(solution)/shard_map/secf,secd->efd/dot_general | solution.py:230
  313.4 4.7 gather_fusion.3
  318.1 19.5 %all-to-all-done.3 = bf16[4,256,768]{2,1,0:T(8,128)(2,1)} async-done(((bf16[4,256,768]{2,1,0:T(8,128)(2,1)}), bf16[4,256,768]{2,1,0:T(8,128)(2,1)}, u32[]{:S(2)}, u32[]{:S(2)}) %all-to-all-start.3) | async-done | bytes 1572896 | tf_op jit(solution)/shard_map/all_to_all | solution.py:241
  337.6 4.7 gather_fusion.5
  342.3 3.1 fusion.102
  345.4 3.7 fusion.100
  356.2 8.6 %fusion.110 = bf16[12,64,512]{2,1,0:T(8,128)(2,1)} fusion(bf16[512,12,64]{0,2,1:T(8,128)(2,1)} %bitcast.311, f32[12,512,512]{1,2,0:T(8,128)} %get-tuple-element.245, f32[12,512]{1,0:T(8,128)} %log_add_fusion, pred[512,512]{0,1:T(8,128)(4,1)} %get-tuple-element.240), kind=kOutput, calls=%fused_computation.132 | convolution fusion | flops 415629312 | bytes 14442496 | tf_op jit(solution)/shard_map/while/body/eval_jaxpr/hqk,qhd->khd/dot_general | solution.py:126
  364.8 7.8 %multiply_convert_fusion = bf16[12,512,512]{1,2,0:T(8,128)(2,1)S(1)} fusion(f32[12,512,512]{1,2,0:T(8,128)} %get-tuple-element.245, f32[12,512]{1,0:T(8,128)S(1)} %bitcast.331, f32[12,512]{1,0:T(8,128)S(1)} %copy-done.47, pred[512,512]{0,1:T(8,128)(4,1)S(1)} %copy-done.22, bf16[512,12,64]{0,2,1:T(8,128)(2,1)S(1)} %bitcast.312, ...), kind=kOutput, calls=%fused_computation.22 | convolution fusion | flops 421527552 | bytes 20758528 | tf_op jit(solution)/shard_map/while/body/eval_jaxpr/qhd,khd->hqk/dot_general | solution.py:96
  372.7 7.6 %multiply_convert_fusion.2 = bf16[12,512,512]{1,2,0:T(8,128)(2,1)S(1)} fusion(f32[12,512,512]{1,2,0:T(8,128)} %get-tuple-element.262, f32[12,512]{1,0:T(8,128)S(1)} %bitcast.332, f32[12,512]{1,0:T(8,128)S(1)} %copy-done.47, pred[512,512]{0,1:T(8,128)(4,1)} %get-tuple-element.239, bf16[512,12,64]{0,2,1:T(8,128)(2,1)S(1)} %bitcast.313, ...), kind=kOutput, calls=%fused_computation.26 | convolution fusion | flops 421527552 | bytes 20758528 | tf_op jit(solution)/shard_map/while/body/eval_jaxpr/qhd,khd->hqk/dot_general | solution.py:96
  380.3 2.4 fusion.160
  382.7 3.1 convolution_multiply_fusion
  385.8 8.0 %multiply_convert_fusion.1 = bf16[12,512,512]{1,2,0:T(8,128)(2,1)S(1)} fusion(f32[12,512,512]{1,2,0:T(8,128)} %get-tuple-element.247, f32[12,512]{1,0:T(8,128)S(1)} %bitcast.333, f32[12,512]{1,0:T(8,128)S(1)} %copy-done.47, pred[512,512]{0,1:T(8,128)(4,1)} %get-tuple-element.241, bf16[512,12,64]{0,2,1:T(8,128)(2,1)S(1)} %bitcast.314, ...), kind=kOutput, calls=%fused_computation.24 | convolution fusion | flops 421527552 | bytes 20758528 | tf_op jit(solution)/shard_map/while/body/eval_jaxpr/qhd,khd->hqk/dot_general | solution.py:96
  398.5 3.1 convolution_multiply_fusion.1
  401.7 2.3 fusion.161
  404.0 6.1 fusion.30
  410.2 3.4 fusion.64
  419.8 3.6 fusion.32
  423.5 14.7 %collective-permute-done.3 = bf16[512,1536]{0,1:T(8,128)(2,1)} collective-permute-done((bf16[512,1536]{0,1:T(8,128)(2,1)}, bf16[512,1536]{0,1:T(8,128)(2,1)}, u32[]{:S(2)}, u32[]{:S(2)}) %collective-permute-start.3) | collective-permute-done | bytes 1572896 | tf_op jit(solution)/shard_map/ppermute | solution.py:17
  441.4 5.3 fusion.106
  446.7 23.3 %all-reduce.8.cloned.1.call-done = (bf16[1,768,3072]{2,1,0:T(8,128)(2,1)}, bf16[1,3072,768]{2,1,0:T(8,128)(2,1)}) async-done(((bf16[1,768,3072]{2,1,0:T(8,128)(2,1)}, bf16[1,3072,768]{2,1,0:T(8,128)(2,1)}), (bf16[1,768,3072]{2,1,0:T(8,128)(2,1)}, bf16[1,3072,768]{2,1,0:T(8,128)(2,1)})) %all-reduce.8.cloned.1.call-update) | async-done | bytes 9437200 | tf_op jit(solution)/shard_map/psum | solution.py:304
  470.0 7.5 %convert_element_type.162 = f32[1,768,3072]{2,1,0:T(8,128)} convert(bf16[1,768,3072]{2,1,0:T(8,128)(2,1)} %get-tuple-element.192) | non-fusion elementwise | flops 2359296 | bytes 14155776 | tf_op jit(solution)/shard_map/convert_element_type | solution.py:304
  477.6 4.5 convert_element_type.165
  482.1 4.2 fusion.96
  486.2 55.8 %all-reduce = (f32[768]{0:T(1024)}, f32[768]{0:T(1024)}, f32[768]{0:T(1024)}, f32[768]{0:T(1024)}) all-reduce(f32[768]{0:T(1024)} %get-tuple-element.167, f32[768]{0:T(1024)} %get-tuple-element.170, f32[768]{0:T(1024)S(1)} %get-tuple-element.165, f32[768]{0:T(1024)S(1)} %copy-done.50), channel_id=1, replica_groups=mesh['seq'=8,'exp'=4] {'seq','exp'}, use_global_device_ids=true, to_apply=%region_23.24 | all-reduce | flops 3072 | bytes 24576 | tf_op jit(solution)/shard_map/psum | solution.py:292
  543.4 4.0 fusion.95
  547.3 129.1 %all-reduce.6.cloned.1.call-done = (f32[768,2304]{1,0:T(8,128)}, f32[768,768]{1,0:T(8,128)}) async-done(((f32[768,2304]{1,0:T(8,128)}, f32[768,768]{1,0:T(8,128)}), (f32[768,2304]{1,0:T(8,128)}, f32[768,768]{1,0:T(8,128)})) %all-reduce.6.cloned.1.call-update) | async-done | bytes 9437200 | tf_op jit(solution)/shard_map/psum | solution.py:292
  676.4 6.6 copy.132
  (207 shorter events, 55.1 us)
Async XLA Ops:
  8.7 4.9 copy-start.48
  10.2 9.6 %copy-start.57 = (s32[1,512]{1,0:T(1,128)S(1)}, s32[1,512]{1,0:T(1,128)}, u32[]{:S(2)}) copy-start(s32[1,512]{1,0:T(1,128)} %param.14) | copy-start | bytes 6148
  16.2 29.7 %collective-permute-start = (bf16[512,1536]{1,0:T(8,128)(2,1)}, bf16[512,1536]{1,0:T(8,128)(2,1)}, u32[]{:S(2)}, u32[]{:S(2)}) collective-permute-start(bf16[512,1536]{1,0:T(8,128)(2,1)} %slice.67), channel_id=1, source_target_pairs={{0,4},{4,8},{8,12},{12,16},{16,20},{20,24},{24,28},{1,5},{5,9},{9,... | collective-permute-start | bytes 4718600 | tf_op jit(solution)/shard_map/ppermute | solution.py:17
  40.5 18.1 %copy-start.44 = (s32[1024]{0:T(1024)}, s32[1024]{0:T(1024)S(1)}, u32[]{:S(2)}) copy-start(s32[1024]{0:T(1024)S(1)} %broadcast_clamp_fusion) | copy-start | bytes 12292
  45.9 44.2 %collective-permute-start.1 = (bf16[512,1536]{1,0:T(8,128)(2,1)}, bf16[512,1536]{1,0:T(8,128)(2,1)}, u32[]{:S(2)}, u32[]{:S(2)}) collective-permute-start(bf16[512,1536]{1,0:T(8,128)(2,1)} %collective-permute-done), channel_id=1, source_target_pairs={{0,4},{4,8},{8,12},{12,16},{16,20},{20,24},{24,28},{1,5},{5,9},{9,... | collective-permute-start | bytes 4718600 | tf_op jit(solution)/shard_map/ppermute | solution.py:17
  97.3 8.1 %copy-start.33 = (f32[12,512]{1,0:T(8,128)S(1)}, f32[12,512]{1,0:T(8,128)}, u32[]{:S(2)}) copy-start(f32[12,512]{1,0:T(8,128)} %get-tuple-element.248) | copy-start | bytes 73732
  97.3 8.1 %copy-start.39 = (f32[12,512]{1,0:T(8,128)S(1)}, f32[12,512]{1,0:T(8,128)}, u32[]{:S(2)}) copy-start(f32[12,512]{1,0:T(8,128)} %get-tuple-element.246) | copy-start | bytes 73732
  97.3 8.8 %copy-start.19 = (pred[512,512]{0,1:T(8,128)(4,1)S(1)}, pred[512,512]{0,1:T(8,128)(4,1)}, u32[]{:S(2)}) copy-start(pred[512,512]{0,1:T(8,128)(4,1)} %get-tuple-element.241) | copy-start | bytes 786436
  105.4 7.9 %copy-start.41 = (f32[12,512]{1,0:T(8,128)}, f32[12,512]{1,0:T(8,128)S(1)}, u32[]{:S(2)}) copy-start(f32[12,512]{1,0:T(8,128)S(1)} %get-tuple-element.244) | copy-start | bytes 73732
  106.1 7.3 %copy-start.38 = (f32[12,512]{1,0:T(8,128)}, f32[12,512]{1,0:T(8,128)S(1)}, u32[]{:S(2)}) copy-start(f32[12,512]{1,0:T(8,128)S(1)} %get-tuple-element.210) | copy-start | bytes 73732
  106.1 28.1 %slice-start = ((s8[12582912]{0:T(1024)(128)(4,1)}), s8[4194304]{0:T(1024)(128)(4,1)S(1)}, s32[]{:S(2)}) async-start(s8[12582912]{0:T(1024)(128)(4,1)} %bitcast.290), calls=%async_computation.6 | async-start | bytes 8388608
  106.1 28.1 %slice-start.1 = ((s8[12582912]{0:T(1024)(128)(4,1)}), s8[4194304]{0:T(1024)(128)(4,1)S(1)}, s32[]{:S(2)}) async-start(s8[12582912]{0:T(1024)(128)(4,1)} %bitcast.290), calls=%async_computation.7 | async-start | bytes 8388608
  113.4 36.4 %copy-start.34 = (f32[12,512]{1,0:T(8,128)}, f32[12,512]{1,0:T(8,128)S(1)}, u32[]{:S(2)}) copy-start(f32[12,512]{1,0:T(8,128)S(1)} %fusion.13) | copy-start | bytes 73732
  113.4 20.8 %slice-start.2 = ((s8[12582912]{0:T(1024)(128)(4,1)}), s8[4194304]{0:T(1024)(128)(4,1)S(1)}, s32[]{:S(2)}) async-start(s8[12582912]{0:T(1024)(128)(4,1)} %bitcast.290), calls=%async_computation.8 | async-start | bytes 8388608
  137.8 12.1 %copy-start.35 = (f32[12,512]{1,0:T(8,128)}, f32[12,512]{1,0:T(8,128)S(1)}, u32[]{:S(2)}) copy-start(f32[12,512]{1,0:T(8,128)S(1)} %fusion.11) | copy-start | bytes 73732
  142.5 7.4 %copy-start.40 = (f32[12,512]{1,0:T(8,128)S(1)}, f32[12,512]{1,0:T(8,128)}, u32[]{:S(2)}) copy-start(f32[12,512]{1,0:T(8,128)} %get-tuple-element.246) | copy-start | bytes 73732
  142.5 7.4 %copy-start.42 = (f32[12,512]{1,0:T(8,128)S(1)}, f32[12,512]{1,0:T(8,128)}, u32[]{:S(2)}) copy-start(f32[12,512]{1,0:T(8,128)} %copy-done.41) | copy-start | bytes 73732
  142.5 7.4 %copy-start.21 = (pred[512,512]{0,1:T(8,128)(4,1)S(1)}, pred[512,512]{0,1:T(8,128)(4,1)}, u32[]{:S(2)}) copy-start(pred[512,512]{0,1:T(8,128)(4,1)} %get-tuple-element.240) | copy-start | bytes 786436
  142.5 7.4 %copy-start.28 = (bf16[512,768]{0,1:T(8,128)(2,1)S(1)}, bf16[512,768]{0,1:T(8,128)(2,1)}, u32[]{:S(2)}) copy-start(bf16[512,768]{0,1:T(8,128)(2,1)} %copy.92) | copy-start | bytes 2359300
  142.5 7.4 %copy-start.37 = (f32[12,512]{1,0:T(8,128)S(1)}, f32[12,512]{1,0:T(8,128)}, u32[]{:S(2)}) copy-start(f32[12,512]{1,0:T(8,128)} %get-tuple-element.196) | copy-start | bytes 73732
  142.5 7.4 %copy-start.62 = (f32[12,64,512]{2,1,0:T(8,128)S(1)}, f32[12,64,512]{2,1,0:T(8,128)}, u32[]{:S(2)}) copy-start(f32[12,64,512]{2,1,0:T(8,128)} %fusion.36) | copy-start | bytes 4718596
  142.5 7.4 %copy-start.63 = (f32[12,64,512]{2,1,0:T(8,128)S(1)}, f32[12,64,512]{2,1,0:T(8,128)}, u32[]{:S(2)}) copy-start(f32[12,64,512]{2,1,0:T(8,128)} %fusion.38) | copy-start | bytes 4718596
  149.9 8.9 %copy-start.36 = (f32[12,512]{1,0:T(8,128)}, f32[12,512]{1,0:T(8,128)S(1)}, u32[]{:S(2)}) copy-start(f32[12,512]{1,0:T(8,128)S(1)} %fusion.15) | copy-start | bytes 73732
  150.0 8.8 %copy-start.10 = (bf16[1,512,768]{2,1,0:T(8,128)(2,1)S(1)}, bf16[1,512,768]{2,1,0:T(8,128)(2,1)}, u32[]{:S(2)}) copy-start(bf16[1,512,768]{2,1,0:T(8,128)(2,1)} %param.13) | copy-start | bytes 2359300
  150.0 8.8 %copy-start.59 = (bf16[768,768]{1,0:T(8,128)(2,1)S(1)}, bf16[768,768]{1,0:T(8,128)(2,1)}, u32[]{:S(2)}) copy-start(bf16[768,768]{1,0:T(8,128)(2,1)} %param.22) | copy-start | bytes 3538948
  173.5 41.0 %all-to-all-start = ((bf16[4,256,768]{2,1,0:T(8,128)(2,1)}), bf16[4,256,768]{2,1,0:T(8,128)(2,1)}, u32[]{:S(2)}, u32[]{:S(2)}) async-start(bf16[4,256,768]{2,1,0:T(8,128)(2,1)} %get-tuple-element.243), calls=%async_computation | async-start | bytes 3145728 | tf_op jit(solution)/shard_map/all_to_all | solution.py:207
  214.5 40.9 %all-to-all-start.2 = ((bf16[4,256,768]{2,1,0:T(8,128)(2,1)}), bf16[4,256,768]{2,1,0:T(8,128)(2,1)}, u32[]{:S(2)}, u32[]{:S(2)}) async-start(bf16[4,256,768]{2,1,0:T(8,128)(2,1)} %get-tuple-element.242), calls=%async_computation.2 | async-start | bytes 3145728 | tf_op jit(solution)/shard_map/all_to_all | solution.py:227
  226.3 4.5 copy-start.64
  255.4 41.3 %all-to-all-start.1 = ((bf16[4,256,768]{2,1,0:T(8,128)(2,1)}), bf16[4,256,768]{2,1,0:T(8,128)(2,1)}, u32[]{:S(2)}, u32[]{:S(2)}) async-start(bf16[4,256,768]{2,1,0:T(8,128)(2,1)} %fusion.77), calls=%async_computation.1 | async-start | bytes 3145728 | tf_op jit(solution)/shard_map/all_to_all | solution.py:215
  296.7 40.9 %all-to-all-start.3 = ((bf16[4,256,768]{2,1,0:T(8,128)(2,1)}), bf16[4,256,768]{2,1,0:T(8,128)(2,1)}, u32[]{:S(2)}, u32[]{:S(2)}) async-start(bf16[4,256,768]{2,1,0:T(8,128)(2,1)} %fusion.82), calls=%async_computation.3 | async-start | bytes 3145728 | tf_op jit(solution)/shard_map/all_to_all | solution.py:241
  301.1 169.0 %all-reduce.8.cloned.1.call-start = ((), (), s32[]{:S(2)}) async-start(), calls=%async_computation.5 | async-start | bytes 18874368 | tf_op jit(solution)/shard_map/psum | solution.py:304
  313.2 363.2 %all-reduce.6.cloned.1.call-start = ((), (), s32[]{:S(2)}) async-start(), calls=%async_computation.4 | async-start | bytes 18874368 | tf_op jit(solution)/shard_map/psum | solution.py:292
  318.1 24.2 %copy-start.46 = (f32[512]{0:T(512)S(1)}, f32[512]{0:T(512)}, u32[]{:S(2)}) copy-start(f32[512]{0:T(512)} %copy-done.45) | copy-start | bytes 6148
  342.3 8.0 %copy-start.60 = (bf16[768,768]{1,0:T(8,128)(2,1)S(1)}, bf16[768,768]{1,0:T(8,128)(2,1)}, u32[]{:S(2)}) copy-start(bf16[768,768]{1,0:T(8,128)(2,1)} %param.22) | copy-start | bytes 3538948
  356.2 8.6 %copy-start.17 = (bf16[512,768]{0,1:T(8,128)(2,1)S(1)}, bf16[512,768]{0,1:T(8,128)(2,1)}, u32[]{:S(2)}) copy-start(bf16[512,768]{0,1:T(8,128)(2,1)} %copy.94) | copy-start | bytes 2359300
  356.2 8.6 %copy-start.22 = (pred[512,512]{0,1:T(8,128)(4,1)S(1)}, pred[512,512]{0,1:T(8,128)(4,1)}, u32[]{:S(2)}) copy-start(pred[512,512]{0,1:T(8,128)(4,1)} %get-tuple-element.240) | copy-start | bytes 786436
  356.2 8.6 %copy-start.29 = (bf16[512,768]{0,1:T(8,128)(2,1)S(1)}, bf16[512,768]{0,1:T(8,128)(2,1)}, u32[]{:S(2)}) copy-start(bf16[512,768]{0,1:T(8,128)(2,1)} %copy.92) | copy-start | bytes 2359300
  356.2 8.6 %copy-start.47 = (f32[12,512]{1,0:T(8,128)S(1)}, f32[12,512]{1,0:T(8,128)}, u32[]{:S(2)}) copy-start(f32[12,512]{1,0:T(8,128)} %log_add_fusion) | copy-start | bytes 73732
  372.7 7.6 %copy-start.8 = (bf16[512,768]{0,1:T(8,128)(2,1)S(1)}, bf16[512,768]{0,1:T(8,128)(2,1)}, u32[]{:S(2)}) copy-start(bf16[512,768]{0,1:T(8,128)(2,1)} %copy.85) | copy-start | bytes 2359300
  397.1 4.6 copy-start.7
  397.1 13.0 %collective-permute-start.2 = (bf16[512,1536]{0,1:T(8,128)(2,1)}, bf16[512,1536]{0,1:T(8,128)(2,1)}, u32[]{:S(2)}, u32[]{:S(2)}) collective-permute-start(bf16[512,1536]{0,1:T(8,128)(2,1)} %pad_maximum_fusion.1), channel_id=1, source_target_pairs={{4,0},{8,4},{12,8},{16,12},{20,16},{24,20},{28,24},{5,1},{9,5},{13... | collective-permute-start | bytes 4718600 | tf_op jit(solution)/shard_map/ppermute | solution.py:17
  404.0 6.1 copy-start.15
  404.0 15.7 %slice-start.3 = ((s8[12582912]{0:T(1024)(128)(4,1)}), s8[4194304]{0:T(1024)(128)(4,1)S(1)}, s32[]{:S(2)}) async-start(s8[12582912]{0:T(1024)(128)(4,1)} %bitcast.292), calls=%async_computation.9 | async-start | bytes 8388608
  404.0 15.7 %slice-start.4 = ((s8[12582912]{0:T(1024)(128)(4,1)}), s8[4194304]{0:T(1024)(128)(4,1)S(1)}, s32[]{:S(2)}) async-start(s8[12582912]{0:T(1024)(128)(4,1)} %bitcast.292), calls=%async_computation.10 | async-start | bytes 8388608
  410.1 5.3 copy-start.4
  410.1 5.3 copy-start.27
  410.2 7.5 %copy-start.5 = (f32[12,64,512]{2,1,0:T(8,128)S(1)}, f32[12,64,512]{2,1,0:T(8,128)}, u32[]{:S(2)}) copy-start(f32[12,64,512]{2,1,0:T(8,128)} %fusion.160) | copy-start | bytes 4718596
  410.2 7.5 %copy-start.6 = (f32[12,64,512]{2,1,0:T(8,128)S(1)}, f32[12,64,512]{2,1,0:T(8,128)}, u32[]{:S(2)}) copy-start(f32[12,64,512]{2,1,0:T(8,128)} %fusion.161) | copy-start | bytes 4718596
  410.2 7.5 %copy-start.9 = (bf16[512,768]{0,1:T(8,128)(2,1)S(1)}, bf16[512,768]{0,1:T(8,128)(2,1)}, u32[]{:S(2)}) copy-start(bf16[512,768]{0,1:T(8,128)(2,1)} %copy.91) | copy-start | bytes 2359300
  413.6 6.1 slice-start.5
  413.6 24.5 %collective-permute-start.3 = (bf16[512,1536]{0,1:T(8,128)(2,1)}, bf16[512,1536]{0,1:T(8,128)(2,1)}, u32[]{:S(2)}, u32[]{:S(2)}) collective-permute-start(bf16[512,1536]{0,1:T(8,128)(2,1)} %fusion.64), channel_id=1, source_target_pairs={{4,0},{8,4},{12,8},{16,12},{20,16},{24,20},{28,24},{5,1},{9,5},{13... | collective-permute-start | bytes 4718600 | tf_op jit(solution)/shard_map/ppermute | solution.py:17
  419.8 18.4 %copy-start.14 = (f32[12,64,512]{2,1,0:T(8,128)S(1)}, f32[12,64,512]{2,1,0:T(8,128)}, u32[]{:S(2)}) copy-start(f32[12,64,512]{2,1,0:T(8,128)} %convolution_multiply_fusion) | copy-start | bytes 4718596
  423.4 17.9 %copy-start.11 = (bf16[1,512,768]{2,1,0:T(8,128)(2,1)S(1)}, bf16[1,512,768]{2,1,0:T(8,128)(2,1)}, u32[]{:S(2)}) copy-start(bf16[1,512,768]{2,1,0:T(8,128)(2,1)} %param.13) | copy-start | bytes 2359300
  423.4 17.9 %copy-start.31 = (bf16[12,64,512]{2,1,0:T(8,128)(2,1)S(1)}, bf16[12,64,512]{2,1,0:T(8,128)(2,1)}, u32[]{:S(2)}) copy-start(bf16[12,64,512]{2,1,0:T(8,128)(2,1)} %multiply_convert_fusion.4) | copy-start | bytes 2359300
  423.4 17.9 %copy-start.49 = (f32[512]{0:T(512)S(1)}, f32[512]{0:T(512)}, u32[]{:S(2)}) copy-start(f32[512]{0:T(512)} %copy-done.48) | copy-start | bytes 6148
  423.4 17.9 %copy-start.52 = (f32[512]{0:T(512)S(1)}, f32[512]{0:T(512)}, u32[]{:S(2)}) copy-start(f32[512]{0:T(512)} %copy-done.51) | copy-start | bytes 6148
  423.4 17.9 %copy-start.54 = (f32[768]{0:T(1024)S(1)}, f32[768]{0:T(1024)}, u32[]{:S(2)}) copy-start(f32[768]{0:T(1024)} %param.17) | copy-start | bytes 9220
  423.4 17.9 %copy-start.61 = (f32[768]{0:T(1024)S(1)}, f32[768]{0:T(1024)}, u32[]{:S(2)}) copy-start(f32[768]{0:T(1024)} %param.18) | copy-start | bytes 9220
  470.0 7.5 %copy-start.16 = (bf16[1,3072,768]{2,1,0:T(8,128)(2,1)S(1)}, bf16[1,3072,768]{2,1,0:T(8,128)(2,1)}, u32[]{:S(2)}) copy-start(bf16[1,3072,768]{2,1,0:T(8,128)(2,1)} %get-tuple-element.193) | copy-start | bytes 14155780
  477.5 4.5 copy-start.12
  477.5 4.5 copy-start.25
  477.5 4.5 copy-start.32
  477.5 4.5 copy-start.55
  676.4 6.6 copy-start.23
  (17 other events, 36.6 us)
Sparse Core Ops, SparseCore 0:
  313.3 156.6 all-reduce.7
  477.5 198.8 all-reduce.5
where the time goes:
time: 699 us; the launch traced here: 692 us
  waiting for transfers between devices  233 us (33%)
  matrix products  196 us (28%)
  local copies, waits for them, and re-layouts  86.4 us (12%)
  other arithmetic  74.9 us (11%)
  blocking collectives  55.8 us (8%)
  starting transfers between devices  29.9 us (4%)
  between operations  15.3 us (2%)
    psum x1, waiting for transfers between devices, on_device(): lax.psum((grad_w_qkv, grad_w_out, grad_first_gain, grad_first_bias, grad_...  129 us
    psum x1, blocking collectives, on_device(): lax.psum((grad_w_qkv, grad_w_out, grad_first_gain, grad_first_bias, grad_...  55.8 us
    dot_general x3, matrix products, step(): jnp.einsum('hqk,khd->qhd', shares.astype(jnp.bfloat16), value_rows, prefe...  34.3 us
    all_to_all x1, waiting for transfers between devices, on_device(): lax.all_to_all(send, 'exp', split_axis=0, concat_axis=0, tiled=True)  28.2 us
    dot_general x3, matrix products, step(): jnp.einsum('qhd,khd->hqk', queries, key_rows, preferred_element_type=jnp....  25.3 us
    dot_general x3, matrix products, backward_core(): jnp.einsum('qhd,khd->hqk', grad_heads, value_rows, preferred_element_type...  23.4 us
    psum x1, waiting for transfers between devices, on_device(): lax.psum(grad_w_up.astype(jnp.bfloat16), 'seq').astype(jnp.float32)  23.3 us
    all_to_all x1, waiting for transfers between devices, on_device(): lax.all_to_all(grad_slots.reshape(experts_total, capacity, width), 'exp',...  19.5 us
  transfers between devices with their start and end apart: 10, of which 7 were waited for; matrix products, arithmetic and copies ran while one was open for 36% of the time, Pallas kernels for 0%

commit v1 on v0

--- a/solution.py
+++ b/solution.py
@@ -301,7 +301,7 @@
         ("seq", "exp"),
     )
     expert_sums = (
-        lax.psum(grad_w_up.astype(jnp.bfloat16), "seq").astype(jnp.float32),
+        jnp.sum(lax.all_gather(grad_w_up.astype(jnp.bfloat16), "seq"), axis=0).astype(jnp.float32),
         lax.psum(grad_w_down.astype(jnp.bfloat16), "seq").astype(jnp.float32),
     )
     return (

time: 699 us -> 773 us (1.11)
  blocking collectives: 55.8 us -> 130 us
  other arithmetic: 74.9 us -> 94.1 us
  matrix products: 196 us -> 186 us
    all_to_all x0 -> x1, blocking collectives: none -> 40.8 us  [on_device(): lax.all_to_all(send, 'exp', split_axis=0, concat_axis=0, tiled=True)]
    psum x1, blocking collectives: 55.8 us -> 88.8 us  [on_device(): lax.psum((grad_w_qkv, grad_w_out, grad_first_gain, grad_first_bias, grad_...]
    all_to_all x1 -> x0, waiting for transfers between devices: 28.2 us -> none  [on_device(): lax.all_to_all(send, 'exp', split_axis=0, concat_axis=0, tiled=True)]
    psum x1, waiting for transfers between devices: 23.3 us -> 0.02 us  [on_device(): lax.psum(grad_w_down.astype(jnp.bfloat16), 'seq').astype(jnp.float32)]
    all_to_all x1, waiting for transfers between devices: 4.43 us -> 23.6 us  [on_device(): lax.all_to_all(expert_out.reshape(experts_total, capacity, width), 'exp',...]
    psum x1, waiting for transfers between devices: 129 us -> 146 us  [on_device(): lax.psum((grad_w_qkv, grad_w_out, grad_first_gain, grad_first_bias, grad_...]
    reduce_sum x0 -> x1, other arithmetic: none -> 16.5 us  [on_device(): jnp.sum(lax.all_gather(grad_w_up.astype(jnp.bfloat16), 'seq'), axis=0)]
    all_to_all x1, waiting for transfers between devices: 13.9 us -> 26.1 us  [on_device(): lax.all_to_all(grad_send, 'exp', split_axis=0, concat_axis=0, tiled=True)]
  transfers between devices with their start and end apart: 10 -> 10, of which waited for: 7 -> 5; matrix products, arithmetic and copies ran while one was open for 36% -> 34% of each run, Pallas kernels for 0% -> 0%
where the time goes in v1:
time: 773 us; the launch traced here: 767 us
  waiting for transfers between devices  231 us (30%)
  matrix products  186 us (24%)
  blocking collectives  130 us (17%)
  other arithmetic  94.1 us (12%)
  local copies, waits for them, and re-layouts  85 us (11%)
  starting transfers between devices  25.1 us (3%)
  between operations  15.1 us (2%)
    psum x1, waiting for transfers between devices, on_device(): lax.psum((grad_w_qkv, grad_w_out, grad_first_gain, grad_first_bias, grad_...  146 us
    psum x1, blocking collectives, on_device(): lax.psum((grad_w_qkv, grad_w_out, grad_first_gain, grad_first_bias, grad_...  88.8 us
    all_to_all x1, blocking collectives, on_device(): lax.all_to_all(send, 'exp', split_axis=0, concat_axis=0, tiled=True)  40.8 us
    all_to_all x1, waiting for transfers between devices, on_device(): lax.all_to_all(grad_send, 'exp', split_axis=0, concat_axis=0, tiled=True)  26.1 us
    dot_general x3, matrix products, step(): jnp.einsum('qhd,khd->hqk', queries, key_rows, preferred_element_type=jnp....  25.1 us
    dot_general x3, matrix products, backward_core(): jnp.einsum('qhd,khd->hqk', grad_heads, value_rows, preferred_element_type...  23.8 us
    all_to_all x1, waiting for transfers between devices, on_device(): lax.all_to_all(expert_out.reshape(experts_total, capacity, width), 'exp',...  23.6 us
    all_to_all x1, waiting for transfers between devices, on_device(): lax.all_to_all(grad_slots.reshape(experts_total, capacity, width), 'exp',...  23.6 us
  transfers between devices with their start and end apart: 10, of which 5 were waited for; matrix products, arithmetic and copies ran while one was open for 34% of the time, Pallas kernels for 0%

profile of v1, /device:TPU:0, one launch (start us, length us, event | category | flops | bytes accessed | tf_op | source)
XLA Modules:
  0.0 766.6 jit_solution(8098123838812625864)
XLA Ops:
  10.2 3.3 convolution_convert_fusion
  16.2 3.5 collective-permute-start
  19.7 3.4 gather_fusion
  23.3 3.8 sort.31
  29.1 11.3 %gather_fusion.1 = s32[1024]{0:T(1024)} fusion(s32[512]{0:T(512)S(1)} %get-tuple-element.163, s32[1024]{0:T(1024)S(1)} %broadcast_clamp_fusion.1), kind=kCustom, calls=%fused_computation.1 | custom fusion | bytes 12288 | tf_op jit(solution)/shard_map/gather | solution.py:202
  41.9 3.1 fusion.152
  47.2 4.5 collective-permute-start.1
  53.0 2.3 copy.84
  55.3 2.3 copy.85
  60.0 7.3 gather_fusion.4
  67.3 8.5 %select_reduce_fusion.2 = (f32[12,512]{1,0:T(8,128)}, f32[12,512,512]{1,2,0:T(8,128)}) fusion(pred[512,512]{0,1:T(8,128)(4,1)} %get-tuple-element.237, bf16[512,12,64]{0,2,1:T(8,128)(2,1)} %bitcast.292, bf16[512,12,64]{0,2,1:T(8,128)(2,1)} %bitcast.299), kind=kOutput, calls=%fused_computation.33 | convolution fusion | flops 412084224 | bytes 14442496 | tf_op jit(solution)/shard_map/while/body/eval_jaxpr/qhd,khd->hqk/dot_general | solution.py:71
  75.8 2.6 fusion.154
  83.0 8.5 %select_reduce_fusion.1 = (f32[12,512]{1,0:T(8,128)}, f32[12,512,512]{1,2,0:T(8,128)}) fusion(pred[512,512]{0,1:T(8,128)(4,1)} %get-tuple-element.239, bf16[512,12,64]{0,2,1:T(8,128)(2,1)} %bitcast.293, bf16[512,12,64]{0,2,1:T(8,128)(2,1)} %bitcast.301), kind=kOutput, calls=%fused_computation.31 | convolution fusion | flops 412084224 | bytes 14442496 | tf_op jit(solution)/shard_map/while/body/eval_jaxpr/qhd,khd->hqk/dot_general | solution.py:71
  91.5 2.6 fusion.153
  94.1 2.3 copy.91
  98.8 8.0 %select_reduce_fusion = (f32[12,512]{1,0:T(8,128)S(1)}, f32[12,512,512]{1,2,0:T(8,128)}) fusion(pred[512,512]{0,1:T(8,128)(4,1)} %get-tuple-element.238, bf16[512,12,64]{0,2,1:T(8,128)(2,1)} %bitcast.294, bf16[512,12,64]{0,2,1:T(8,128)(2,1)} %bitcast.303), kind=kOutput, calls=%fused_computation.29 | convolution fusion | flops 412084224 | bytes 14442496 | tf_op jit(solution)/shard_map/while/body/eval_jaxpr/qhd,khd->hqk/dot_general | solution.py:71
  107.4 7.3 fusion.13
  114.7 8.7 %fusion.36 = f32[12,64,512]{2,1,0:T(8,128)} fusion(bf16[512,12,64]{0,2,1:T(8,128)(2,1)} %bitcast.323, f32[12,512,512]{1,2,0:T(8,128)} %get-tuple-element.245, f32[12,512]{1,0:T(8,128)S(1)} %get-tuple-element.195, pred[512,512]{0,1:T(8,128)(4,1)} %get-tuple-element.239), kind=kOutput, calls=%fused_computation.57 | convolution fusion | flops 415236096 | bytes 15228928 | tf_op jit(solution)/shard_map/while/body/eval_jaxpr/hqk,khd->qhd/dot_general | solution.py:78
  123.5 3.5 fusion.11
  127.0 4.7 fusion.38
  131.8 7.3 fusion.15
  139.3 8.8 %fusion.155 = (bf16[512,12,64]{0,2,1:T(8,128)(2,1)S(1)}, f32[512,12,64]{0,2,1:T(8,128)}) fusion(f32[512,12]{0,1:T(8,128)S(1)} %get-tuple-element.192, bf16[512,12,64]{0,2,1:T(8,128)(2,1)S(1)} %bitcast.326, f32[12,512,512]{1,2,0:T(8,128)} %get-tuple-element.243, f32[12,512]{1,0:T(8,128)S(1)} %copy-done.34, pred[512,512]{0,1:T(8,128)(4,1)S(1)} %copy-done.19, ...), kind=kOutput, calls=%fused_computation.216 | convolution fusion | flops 417988608 | bytes 19259392 | tf_op jit(solution)/shard_map/while/body/eval_jaxpr/hqk,khd->qhd/dot_general | solution.py:78
  151.9 7.0 gather_fusion.2
  158.9 3.3 broadcast_select_fusion
  162.3 40.8 %all_to_all.20 = bf16[4,256,768]{2,1,0:T(8,128)(2,1)} all-to-all(bf16[4,256,768]{2,1,0:T(8,128)(2,1)S(1)} %get-tuple-element.241), channel_id=1, replica_groups=mesh['seq'=8,'exp'=4] {'exp'}, dimensions={0} | all-to-all | bytes 3145728 | tf_op jit(solution)/shard_map/all_to_all | solution.py:207
  203.1 4.4 all-to-all-start.2
  207.5 10.0 %fusion.54 = f32[4,256,3072]{2,1,0:T(8,128)} fusion(bf16[4,256,768]{2,1,0:T(8,128)(2,1)} %all_to_all.20, bf16[1,768,3072]{2,1,0:T(8,128)(2,1)} %param.23), kind=kOutput, calls=%fused_computation.70 | convolution fusion | flops 4831838208 | bytes 18874368 | tf_op jit(solution)/shard_map/secd,edf->secf/dot_general | solution.py:209
  217.5 26.1 %all-to-all-done.2 = bf16[4,256,768]{2,1,0:T(8,128)(2,1)} async-done(((bf16[4,256,768]{2,1,0:T(8,128)(2,1)}), bf16[4,256,768]{2,1,0:T(8,128)(2,1)}, u32[]{:S(2)}, u32[]{:S(2)}) %all-to-all-start.2) | async-done | bytes 1572896 | tf_op jit(solution)/shard_map/all_to_all | solution.py:227
  243.6 12.0 %fusion.56 = bf16[1,3072,768]{2,1,0:T(8,128)(2,1)} fusion(bf16[4,256,768]{2,1,0:T(8,128)(2,1)} %all-to-all-done.2, f32[4,256,3072]{2,1,0:T(8,128)} %fusion.54), kind=kOutput, calls=%fused_computation.72 | convolution fusion | flops 4862509056 | bytes 18874368 | tf_op jit(solution)/shard_map/secf,secd->efd/dot_general | solution.py:230
  256.1 15.8 %fusion.6 = bf16[4,1,256,3072]{3,2,0,1:T(8,128)(2,1)S(1)} fusion(f32[4,256,3072]{2,1,0:T(8,128)} %fusion.54, bf16[4,256,768]{2,1,0:T(8,128)(2,1)} %all-to-all-done.2, bf16[1,3072,768]{2,1,0:T(8,128)(2,1)} %param.24), kind=kOutput, calls=%fused_computation.14 | convolution fusion | flops 4894752768 | bytes 25165824 | tf_op jit(solution)/shard_map/secd,efd->secf/dot_general | solution.py:233
  271.9 2.7 copy-done.61
  274.6 6.8 bitcast_convert_fusion.1
  281.5 9.6 %fusion.79 = bf16[4,256,768]{2,1,0:T(8,128)(2,1)} fusion(bf16[1,768,3072]{2,1,0:T(8,128)(2,1)} %param.23, bf16[4,1,256,3072]{3,2,0,1:T(8,128)(2,1)} %copy-done.61), kind=kOutput, calls=%fused_computation.96 | convolution fusion | flops 4832624640 | bytes 12582912 | tf_op jit(solution)/shard_map/secf,edf->secd/dot_general | solution.py:238
  291.0 4.3 all-to-all-start.3
  295.4 12.6 %fusion.74 = bf16[4,256,768]{2,1,0:T(8,128)(2,1)} fusion(bf16[1,3072,768]{2,1,0:T(8,128)(2,1)} %param.24, f32[4,256,3072]{2,1,0:T(8,128)} %fusion.54), kind=kOutput, calls=%fused_computation.95 | convolution fusion | flops 4860936192 | bytes 18874368 | tf_op jit(solution)/shard_map/secf,efd->secd/dot_general | solution.py:212
  308.0 23.6 %all-to-all-done.3 = bf16[4,256,768]{2,1,0:T(8,128)(2,1)} async-done(((bf16[4,256,768]{2,1,0:T(8,128)(2,1)}), bf16[4,256,768]{2,1,0:T(8,128)(2,1)}, u32[]{:S(2)}, u32[]{:S(2)}) %all-to-all-start.3) | async-done | bytes 1572896 | tf_op jit(solution)/shard_map/all_to_all | solution.py:241
  331.6 4.4 all-to-all-start.1
  336.8 4.4 sort.32
  344.2 4.7 gather_fusion.5
  348.9 23.6 %all-to-all-done.1 = bf16[4,256,768]{2,1,0:T(8,128)(2,1)} async-done(((bf16[4,256,768]{2,1,0:T(8,128)(2,1)}), bf16[4,256,768]{2,1,0:T(8,128)(2,1)}, u32[]{:S(2)}, u32[]{:S(2)}) %all-to-all-start.1) | async-done | bytes 1572896 | tf_op jit(solution)/shard_map/all_to_all | solution.py:215
  372.5 4.7 gather_fusion.3
  377.2 3.1 fusion.99
  380.3 3.6 fusion.97
  390.9 9.3 %multiply_convert_fusion = bf16[12,512,512]{1,2,0:T(8,128)(2,1)S(1)} fusion(f32[12,512,512]{1,2,0:T(8,128)} %get-tuple-element.243, f32[12,512]{1,0:T(8,128)S(1)} %bitcast.330, f32[12,512]{1,0:T(8,128)} %log_add_fusion, pred[512,512]{0,1:T(8,128)(4,1)} %get-tuple-element.238, bf16[512,12,64]{0,2,1:T(8,128)(2,1)} %bitcast.310, bf16[512,12,64]{0,2,1:T(8,128)(2,1)} %bitcast.325), kind=kOutput, calls=%fused_computation.22 | convolution fusion | flops 421527552 | bytes 20758528 | tf_op jit(solution)/shard_map/while/body/eval_jaxpr/qhd,khd->hqk/dot_general | solution.py:96
  402.2 6.1 fusion.107
  411.1 7.3 multiply_convert_fusion.2
  418.4 3.1 convolution_multiply_fusion
  421.5 2.3 fusion.157
  423.9 7.3 multiply_convert_fusion.1
  431.1 3.1 convolution_multiply_fusion.1
  434.3 2.4 fusion.158
  436.7 6.1 fusion.30
  442.9 3.4 fusion.61
  452.5 3.6 fusion.32
  456.1 11.7 %collective-permute-done.3 = bf16[512,1536]{0,1:T(8,128)(2,1)} collective-permute-done((bf16[512,1536]{0,1:T(8,128)(2,1)}, bf16[512,1536]{0,1:T(8,128)(2,1)}, u32[]{:S(2)}, u32[]{:S(2)}) %collective-permute-start.3) | collective-permute-done | bytes 1572896 | tf_op jit(solution)/shard_map/ppermute | solution.py:17
  471.0 5.3 fusion.103
  476.4 7.0 convert_element_type.176
  483.4 4.2 fusion.93
  487.6 88.8 %all-reduce = (f32[768]{0:T(1024)}, f32[768]{0:T(1024)}, f32[768]{0:T(1024)}, f32[768]{0:T(1024)}) all-reduce(f32[768]{0:T(1024)} %get-tuple-element.167, f32[768]{0:T(1024)} %get-tuple-element.170, f32[768]{0:T(1024)S(1)} %get-tuple-element.165, f32[768]{0:T(1024)S(1)} %copy-done.47), channel_id=1, replica_groups=mesh['seq'=8,'exp'=4] {'seq','exp'}, use_global_device_ids=true, to_apply=%region_23.24 | all-reduce | flops 3072 | bytes 24576 | tf_op jit(solution)/shard_map/psum | solution.py:292
  577.7 3.9 fusion.92
  581.6 16.5 %reduce.3 = bf16[768,3072]{1,0:T(8,128)(2,1)} reduce(bf16[8,768,3072]{2,1,0:T(8,128)(2,1)} %bitcast.298, bf16[]{:T(256)} %constant.135.clone.1), dimensions={0}, to_apply=%region_30.31 | reduce | flops 16515072 | bytes 42467328 | tf_op jit(solution)/shard_map/reduce_sum | solution.py:304
  598.1 7.4 bitcast_convert_fusion.2
  605.5 146.1 %all-reduce.7.cloned.1.call-done = (f32[768,2304]{1,0:T(8,128)}, f32[768,768]{1,0:T(8,128)}) async-done(((f32[768,2304]{1,0:T(8,128)}, f32[768,768]{1,0:T(8,128)}), (f32[768,2304]{1,0:T(8,128)}, f32[768,768]{1,0:T(8,128)})) %all-reduce.7.cloned.1.call-update) | async-done | bytes 9437200 | tf_op jit(solution)/shard_map/psum | solution.py:292
  751.6 6.6 copy.131
  (204 shorter events, 54.7 us)
Async XLA Ops:
  7.2 3.0 copy-start
  8.7 4.9 copy-start.45
  10.2 3.3 copy-start.48
  10.2 9.5 %copy-start.54 = (s32[1,512]{1,0:T(1,128)S(1)}, s32[1,512]{1,0:T(1,128)}, u32[]{:S(2)}) copy-start(s32[1,512]{1,0:T(1,128)} %param.14) | copy-start | bytes 6148
  16.2 31.0 %collective-permute-start = (bf16[512,1536]{1,0:T(8,128)(2,1)}, bf16[512,1536]{1,0:T(8,128)(2,1)}, u32[]{:S(2)}, u32[]{:S(2)}) collective-permute-start(bf16[512,1536]{1,0:T(8,128)(2,1)} %slice.67), channel_id=1, source_target_pairs={{0,4},{4,8},{8,12},{12,16},{16,20},{20,24},{24,28},{1,5},{5,9},{9,... | collective-permute-start | bytes 4718600 | tf_op jit(solution)/shard_map/ppermute | solution.py:17
  23.3 5.8 copy-start.55
  41.9 18.1 %copy-start.41 = (s32[1024]{0:T(1024)}, s32[1024]{0:T(1024)S(1)}, u32[]{:S(2)}) copy-start(s32[1024]{0:T(1024)S(1)} %broadcast_clamp_fusion) | copy-start | bytes 12292
  47.2 44.3 %collective-permute-start.1 = (bf16[512,1536]{1,0:T(8,128)(2,1)}, bf16[512,1536]{1,0:T(8,128)(2,1)}, u32[]{:S(2)}, u32[]{:S(2)}) collective-permute-start(bf16[512,1536]{1,0:T(8,128)(2,1)} %collective-permute-done), channel_id=1, source_target_pairs={{0,4},{4,8},{8,12},{12,16},{16,20},{20,24},{24,28},{1,5},{5,9},{9,... | collective-permute-start | bytes 4718600 | tf_op jit(solution)/shard_map/ppermute | solution.py:17
  98.8 8.0 %copy-start.30 = (f32[12,512]{1,0:T(8,128)S(1)}, f32[12,512]{1,0:T(8,128)}, u32[]{:S(2)}) copy-start(f32[12,512]{1,0:T(8,128)} %get-tuple-element.246) | copy-start | bytes 73732
  98.8 8.0 %copy-start.36 = (f32[12,512]{1,0:T(8,128)S(1)}, f32[12,512]{1,0:T(8,128)}, u32[]{:S(2)}) copy-start(f32[12,512]{1,0:T(8,128)} %get-tuple-element.244) | copy-start | bytes 73732
  98.8 8.6 %copy-start.17 = (pred[512,512]{0,1:T(8,128)(4,1)S(1)}, pred[512,512]{0,1:T(8,128)(4,1)}, u32[]{:S(2)}) copy-start(pred[512,512]{0,1:T(8,128)(4,1)} %get-tuple-element.239) | copy-start | bytes 786436
  106.8 7.9 %copy-start.38 = (f32[12,512]{1,0:T(8,128)}, f32[12,512]{1,0:T(8,128)S(1)}, u32[]{:S(2)}) copy-start(f32[12,512]{1,0:T(8,128)S(1)} %get-tuple-element.242) | copy-start | bytes 73732
  107.4 7.3 copy-start.35
  107.4 16.1 %slice-start = ((s8[12582912]{0:T(1024)(128)(4,1)}), s8[4194304]{0:T(1024)(128)(4,1)S(1)}, s32[]{:S(2)}) async-start(s8[12582912]{0:T(1024)(128)(4,1)} %bitcast.288), calls=%async_computation.7 | async-start | bytes 8388608
  107.4 16.1 %slice-start.1 = ((s8[12582912]{0:T(1024)(128)(4,1)}), s8[4194304]{0:T(1024)(128)(4,1)S(1)}, s32[]{:S(2)}) async-start(s8[12582912]{0:T(1024)(128)(4,1)} %bitcast.288), calls=%async_computation.8 | async-start | bytes 8388608
  114.7 24.4 %copy-start.31 = (f32[12,512]{1,0:T(8,128)}, f32[12,512]{1,0:T(8,128)S(1)}, u32[]{:S(2)}) copy-start(f32[12,512]{1,0:T(8,128)S(1)} %fusion.13) | copy-start | bytes 73732
  114.7 8.7 %slice-start.2 = ((s8[12582912]{0:T(1024)(128)(4,1)}), s8[4194304]{0:T(1024)(128)(4,1)S(1)}, s32[]{:S(2)}) async-start(s8[12582912]{0:T(1024)(128)(4,1)} %bitcast.288), calls=%async_computation.9 | async-start | bytes 8388608
  127.0 12.1 %copy-start.32 = (f32[12,512]{1,0:T(8,128)}, f32[12,512]{1,0:T(8,128)S(1)}, u32[]{:S(2)}) copy-start(f32[12,512]{1,0:T(8,128)S(1)} %fusion.11) | copy-start | bytes 73732
  131.8 7.4 copy-start.37
  131.8 7.4 copy-start.39
  131.8 7.4 copy-start.19
  131.8 7.4 copy-start.27
  131.8 7.4 copy-start.34
  131.8 7.4 copy-start.59
  131.8 7.4 copy-start.60
  139.2 8.9 %copy-start.33 = (f32[12,512]{1,0:T(8,128)}, f32[12,512]{1,0:T(8,128)S(1)}, u32[]{:S(2)}) copy-start(f32[12,512]{1,0:T(8,128)S(1)} %fusion.15) | copy-start | bytes 73732
  139.2 8.8 %copy-start.10 = (bf16[1,512,768]{2,1,0:T(8,128)(2,1)S(1)}, bf16[1,512,768]{2,1,0:T(8,128)(2,1)}, u32[]{:S(2)}) copy-start(bf16[1,512,768]{2,1,0:T(8,128)(2,1)} %param.13) | copy-start | bytes 2359300
  139.3 8.8 %copy-start.56 = (bf16[768,768]{1,0:T(8,128)(2,1)S(1)}, bf16[768,768]{1,0:T(8,128)(2,1)}, u32[]{:S(2)}) copy-start(bf16[768,768]{1,0:T(8,128)(2,1)} %param.22) | copy-start | bytes 3538948
  203.1 40.5 %all-to-all-start.2 = ((bf16[4,256,768]{2,1,0:T(8,128)(2,1)}), bf16[4,256,768]{2,1,0:T(8,128)(2,1)}, u32[]{:S(2)}, u32[]{:S(2)}) async-start(bf16[4,256,768]{2,1,0:T(8,128)(2,1)} %get-tuple-element.240), calls=%async_computation.2 | async-start | bytes 3145728 | tf_op jit(solution)/shard_map/all_to_all | solution.py:227
  207.4 268.9 %all-reduce.5.cloned.1.call-start = ((), (), s32[]{:S(2)}) async-start(), calls=%async_computation.4 | async-start | bytes 9437184 | tf_op jit(solution)/shard_map/psum | solution.py:305
  255.6 326.0 %all-gather.3.cloned.1.call-start = ((), (), s32[]{:S(2)}) async-start(), calls=%async_computation.5 | async-start | bytes 42467328 | tf_op jit(solution)/shard_map/all_gather | solution.py:304
  256.1 18.6 %copy-start.22 = (bf16[4,256,768]{2,1,0:T(8,128)(2,1)S(1)}, bf16[4,256,768]{2,1,0:T(8,128)(2,1)}, u32[]{:S(2)}) copy-start(bf16[4,256,768]{2,1,0:T(8,128)(2,1)} %all_to_all.20) | copy-start | bytes 4718596
  291.0 40.6 %all-to-all-start.3 = ((bf16[4,256,768]{2,1,0:T(8,128)(2,1)}), bf16[4,256,768]{2,1,0:T(8,128)(2,1)}, u32[]{:S(2)}, u32[]{:S(2)}) async-start(bf16[4,256,768]{2,1,0:T(8,128)(2,1)} %fusion.79), calls=%async_computation.3 | async-start | bytes 3145728 | tf_op jit(solution)/shard_map/all_to_all | solution.py:241
  331.6 40.9 %all-to-all-start.1 = ((bf16[4,256,768]{2,1,0:T(8,128)(2,1)}), bf16[4,256,768]{2,1,0:T(8,128)(2,1)}, u32[]{:S(2)}, u32[]{:S(2)}) async-start(bf16[4,256,768]{2,1,0:T(8,128)(2,1)} %fusion.74), calls=%async_computation.1 | async-start | bytes 3145728 | tf_op jit(solution)/shard_map/all_to_all | solution.py:215
  336.0 415.6 %all-reduce.7.cloned.1.call-start = ((), (), s32[]{:S(2)}) async-start(), calls=%async_computation.6 | async-start | bytes 18874368 | tf_op jit(solution)/shard_map/psum | solution.py:292
  348.9 28.3 %copy-start.43 = (f32[512]{0:T(512)S(1)}, f32[512]{0:T(512)}, u32[]{:S(2)}) copy-start(f32[512]{0:T(512)} %copy-done.42) | copy-start | bytes 6148
  377.2 7.8 %copy-start.57 = (bf16[768,768]{1,0:T(8,128)(2,1)S(1)}, bf16[768,768]{1,0:T(8,128)(2,1)}, u32[]{:S(2)}) copy-start(bf16[768,768]{1,0:T(8,128)(2,1)} %param.22) | copy-start | bytes 3538948
  390.9 9.3 %copy-start.1 = (bf16[512,768]{0,1:T(8,128)(2,1)S(1)}, bf16[512,768]{0,1:T(8,128)(2,1)}, u32[]{:S(2)}) copy-start(bf16[512,768]{0,1:T(8,128)(2,1)} %copy.84) | copy-start | bytes 2359300
  409.6 33.2 %collective-permute-start.2 = (bf16[512,1536]{0,1:T(8,128)(2,1)}, bf16[512,1536]{0,1:T(8,128)(2,1)}, u32[]{:S(2)}, u32[]{:S(2)}) collective-permute-start(bf16[512,1536]{0,1:T(8,128)(2,1)} %pad_maximum_fusion.1), channel_id=1, source_target_pairs={{4,0},{8,4},{12,8},{16,12},{20,16},{24,20},{28,24},{5,1},{9,5},{13... | collective-permute-start | bytes 4718600 | tf_op jit(solution)/shard_map/ppermute | solution.py:17
  418.4 3.2 copy-start.7
  431.1 3.2 copy-start.8
  436.7 6.1 copy-start.15
  436.7 15.8 %slice-start.3 = ((s8[12582912]{0:T(1024)(128)(4,1)}), s8[4194304]{0:T(1024)(128)(4,1)S(1)}, s32[]{:S(2)}) async-start(s8[12582912]{0:T(1024)(128)(4,1)} %bitcast.290), calls=%async_computation.10 | async-start | bytes 8388608
  436.7 15.8 %slice-start.4 = ((s8[12582912]{0:T(1024)(128)(4,1)}), s8[4194304]{0:T(1024)(128)(4,1)S(1)}, s32[]{:S(2)}) async-start(s8[12582912]{0:T(1024)(128)(4,1)} %bitcast.290), calls=%async_computation.11 | async-start | bytes 8388608
  442.8 5.3 copy-start.4
  442.8 5.3 copy-start.26
  442.8 7.5 copy-start.5
  442.8 7.4 copy-start.6
  442.8 7.4 copy-start.9
  446.3 6.2 slice-start.5
  446.3 21.6 %collective-permute-start.3 = (bf16[512,1536]{0,1:T(8,128)(2,1)}, bf16[512,1536]{0,1:T(8,128)(2,1)}, u32[]{:S(2)}, u32[]{:S(2)}) collective-permute-start(bf16[512,1536]{0,1:T(8,128)(2,1)} %fusion.61), channel_id=1, source_target_pairs={{4,0},{8,4},{12,8},{16,12},{20,16},{24,20},{28,24},{5,1},{9,5},{13... | collective-permute-start | bytes 4718600 | tf_op jit(solution)/shard_map/ppermute | solution.py:17
  452.4 15.4 %copy-start.14 = (f32[12,64,512]{2,1,0:T(8,128)S(1)}, f32[12,64,512]{2,1,0:T(8,128)}, u32[]{:S(2)}) copy-start(f32[12,64,512]{2,1,0:T(8,128)} %convolution_multiply_fusion) | copy-start | bytes 4718596
  456.1 14.9 %copy-start.11 = (bf16[1,512,768]{2,1,0:T(8,128)(2,1)S(1)}, bf16[1,512,768]{2,1,0:T(8,128)(2,1)}, u32[]{:S(2)}) copy-start(bf16[1,512,768]{2,1,0:T(8,128)(2,1)} %param.13) | copy-start | bytes 2359300
  456.1 14.9 %copy-start.28 = (bf16[12,64,512]{2,1,0:T(8,128)(2,1)S(1)}, bf16[12,64,512]{2,1,0:T(8,128)(2,1)}, u32[]{:S(2)}) copy-start(bf16[12,64,512]{2,1,0:T(8,128)(2,1)} %multiply_convert_fusion.4) | copy-start | bytes 2359300
  456.1 14.9 %copy-start.46 = (f32[512]{0:T(512)S(1)}, f32[512]{0:T(512)}, u32[]{:S(2)}) copy-start(f32[512]{0:T(512)} %copy-done.45) | copy-start | bytes 6148
  456.1 14.9 %copy-start.49 = (f32[512]{0:T(512)S(1)}, f32[512]{0:T(512)}, u32[]{:S(2)}) copy-start(f32[512]{0:T(512)} %copy-done.48) | copy-start | bytes 6148
  456.1 14.9 %copy-start.51 = (f32[768]{0:T(1024)S(1)}, f32[768]{0:T(1024)}, u32[]{:S(2)}) copy-start(f32[768]{0:T(1024)} %param.17) | copy-start | bytes 9220
  456.1 14.9 %copy-start.58 = (f32[768]{0:T(1024)S(1)}, f32[768]{0:T(1024)}, u32[]{:S(2)}) copy-start(f32[768]{0:T(1024)} %param.18) | copy-start | bytes 9220
  476.3 7.0 copy-start.12
  476.4 7.0 copy-start.24
  476.4 7.0 copy-start.29
  476.4 7.0 copy-start.52
  483.4 4.2 copy-start.47
  751.6 6.6 copy-start.21
  (14 other events, 23.5 us)
Sparse Core Ops, SparseCore 0:
  255.7 85.3 all-reduce.4
  343.8 209.0 all-gather.2
  560.4 191.1 all-reduce.6
